TPU v7x, 32 devices: a whole 2x2x4 slice. The times are simulated.
32 devices in a mesh: groups: 2 (over x), tensor: 16 (over z, y, core).
Axes of the slice: x: 2, y: 2, z: 4, core: 2. Of those that a mesh axis runs over, the one named last changes fastest.
Arguments:
- tokens: bfloat16 [64, 8192], P(('groups', 'tensor')), parts along dimension 0, may hold values from -6 to 6
- gate_weight: bfloat16 [8192, 28672], P(None, 'tensor'), may hold values from -0.0625 to 0.0625
- up_weight: bfloat16 [8192, 28672], P(None, 'tensor'), may hold values from -0.0625 to 0.0625
- down_weight: bfloat16 [28672, 8192], P('tensor'), may hold values from -0.03125 to 0.03125
Outputs:
- mixed: bfloat16 [64, 8192], P(('groups', 'tensor')), parts along dimension 0
There are 2 independent parts, one for each index of `groups`. A program takes and returns all parts, laid end to end along the dimension named above; an argument that names none is the same for every part. Nothing has to cross between parts.
All inputs are finite; a program needn't handle non-finite values.
Results may differ from a plain program's by a relative error of at most 0.015.
Values may be sent and summed in bfloat16 or wider, within the bound.
A program may use at most 128 MiB of HBM per device.

v0:
```python
import jax
import jax.numpy as jnp
import numpy as np
from jax import lax
from jax.sharding import PartitionSpec as P

BLOCK = 32


def swapped(value, axis, stride):
    mask = 2**stride
    pairs = [(source, source ^ mask) for source in range(lax.axis_size(axis))]
    return lax.ppermute(value, axis, pairs)


def walsh(order):
    index = np.arange(order)
    common = index[:, None] & index[None, :]
    parity = common * 0
    for shift in range(max(order.bit_length(), 1)):
        parity = parity ^ common >> shift & 1
    return (1 - 2 * parity).astype(np.float32)


def per_device(tokens, gate_weight, up_weight, down_weight):
    devices = lax.axis_size("tensor")
    width = gate_weight.shape[1]
    scale = 1.0 / np.sqrt(devices * BLOCK)
    inner = jnp.asarray(walsh(BLOCK), jnp.float32)
    piece = lax.all_gather(tokens, "tensor", axis=0, tiled=True)
    gate = jnp.dot(piece, gate_weight, preferred_element_type=jnp.float32)
    up = jnp.dot(piece, up_weight, preferred_element_type=jnp.float32)
    hidden = jax.nn.silu(gate) * up
    total = hidden.shape[0]
    local = jnp.einsum(
        "tbr,rs->tbs",
        hidden.reshape(total, width // BLOCK, BLOCK),
        inner,
        precision=lax.Precision.HIGHEST,
    ).reshape(total, width)
    index = lax.axis_index("tensor")
    for level in range(devices.bit_length() - 1):
        partner = swapped(local.astype(jnp.bfloat16), "tensor", level).astype(local.dtype)
        upper = index // (1 << level) % 2
        local = jnp.where(upper == 1, partner - local, local + partner)
    rotated = (local * scale).astype(jnp.bfloat16)
    terms = jnp.dot(rotated, down_weight, preferred_element_type=jnp.float32)
    mixed = lax.psum_scatter(terms, "tensor", scatter_dimension=0, tiled=True)
    return mixed.astype(jnp.bfloat16)


def solution(mesh):
    return jax.shard_map(
        per_device,
        mesh=mesh,
        in_specs=(
            P(("groups", "tensor"), None),
            P(None, "tensor"),
            P(None, "tensor"),
            P("tensor", None),
        ),
        out_specs=P(("groups", "tensor"), None),
        check_vma=False,
    )
```

profile of v0, /device:TPU:0, one launch (start us, length us, event | category | flops | bytes accessed | tf_op | source)
XLA Modules:
  0.0 150.9 jit_solution(9514124808251258983)
XLA Ops:
  0.0 24.8 %all-gather = bf16[16,2,8192]{2,1,0:T(2,128)(2,1)S(1)} all-gather(bf16[1,2,8192]{2,1,0:T(2,128)(2,1)} %bitcast.10), channel_id=1, replica_groups=mesh['groups'=2,'tensor'=16] {'tensor'}, dimensions={0}, use_global_device_ids=true | all-gather | bytes 557056 | tf_op jit(solution)/shard_map/all_gather | solution.py:30
  24.8 0.2 reshape.9
  25.0 0.0 copy-start
  25.0 11.9 %fusion.16 = f32[32,1792]{1,0:T(8,128)S(1)} fusion(bf16[32,8192]{1,0:T(8,128)(2,1)S(1)} %reshape.9, bf16[8192,1792]{1,0:T(8,128)(2,1)} %param.6), kind=kOutput, calls=%fused_computation.24 | convolution fusion | flops 939524096 | bytes 30113792 | tf_op jit(solution)/shard_map/dot_general | solution.py:31
  36.9 0.0 copy-start.1
  36.9 12.0 %convolution_multiply_fusion = f32[32,1792]{1,0:T(8,128)S(1)} fusion(bf16[32,8192]{1,0:T(8,128)(2,1)S(1)} %reshape.9, bf16[8192,1792]{1,0:T(8,128)(2,1)} %param.7, f32[32,1792]{1,0:T(8,128)S(1)} %fusion.16), kind=kOutput, calls=%fused_computation | convolution fusion | flops 939810816 | bytes 30343168 | tf_op jit(solution)/shard_map/dot_general | solution.py:32
  48.9 0.3 reshape.6
  49.2 0.0 copy-done
  49.3 0.9 fusion.17
  50.1 0.3 reshape.7
  50.4 0.4 collective-permute-start
  50.8 1.0 collective-permute-done
  51.8 0.1 collective-permute-start.1
  51.9 5.4 %collective-permute-done.1 = bf16[32,1792]{1,0:T(8,128)(2,1)S(1)} collective-permute-done((bf16[32,1792]{1,0:T(8,128)(2,1)S(1)}, bf16[32,1792]{1,0:T(8,128)(2,1)S(1)}, u32[]{:S(2)}, u32[]{:S(2)}) %collective-permute-start.1) | collective-permute-done | bytes 114720 | tf_op jit(solution)/shard_map/ppermute | solution.py:13
  57.3 0.1 fusion.14
  57.4 0.1 collective-permute-start.2
  57.5 4.7 %collective-permute-done.2 = bf16[32,1792]{1,0:T(8,128)(2,1)S(1)} collective-permute-done((bf16[32,1792]{1,0:T(8,128)(2,1)S(1)}, bf16[32,1792]{1,0:T(8,128)(2,1)S(1)}, u32[]{:S(2)}, u32[]{:S(2)}) %collective-permute-start.2) | collective-permute-done | bytes 114720 | tf_op jit(solution)/shard_map/ppermute | solution.py:13
  62.3 0.1 collective-permute-start.3
  62.4 0.0 copy-done.1
  62.4 0.6 dynamic-slice
  63.6 5.5 %collective-permute-done.3 = bf16[32,1792]{1,0:T(8,128)(2,1)S(1)} collective-permute-done((bf16[32,1792]{1,0:T(8,128)(2,1)S(1)}, bf16[32,1792]{1,0:T(8,128)(2,1)S(1)}, u32[]{:S(2)}, u32[]{:S(2)}) %collective-permute-start.3) | collective-permute-done | bytes 114720 | tf_op jit(solution)/shard_map/ppermute | solution.py:13
  69.1 11.9 %fusion.8 = f32[32,8192]{1,0:T(8,128)S(1)} fusion(bf16[1792,8192]{1,0:T(8,128)(2,1)} %param.8, bf16[32,1792]{1,0:T(8,128)(2,1)S(1)} %collective-permute-done.3, f32[32,1792]{1,0:T(8,128)S(1)} %get-tuple-element.6, bf16[32,1792]{1,0:T(8,128)(2,1)S(1)} %collective-permute-done.2, pred[]{:T(512)S(6)} %eq.18, pred[]{:T(512)S(6)} %eq.17), kind=kOutput, calls=%fused_computation.17 | convolution fusion | flops 940097536 | bytes 30867458 | tf_op jit(solution)/shard_map/dot_general | solution.py:47
  81.0 69.2 %all-reduce.2 = bf16[32,8192]{1,0:T(8,128)(2,1)S(1)} all-reduce(f32[32,8192]{1,0:T(8,128)S(1)} %fusion.8), channel_id=2, replica_groups=mesh['groups'=2,'tensor'=16] {'tensor'}, use_global_device_ids=true, to_apply=%region_0.1.clone | all-reduce | flops 262144 | bytes 1572864
  150.3 0.7 dynamic-slice_convert_fusion
  (3 shorter events, 0.1 us)
Async XLA Ops:
  25.0 24.2 %copy-start = (f32[32,32,1]{0,1,2:T(8,128)S(1)}, f32[32,32,1]{0,1,2:T(8,128)}, u32[]{:S(2)}) copy-start(f32[32,32,1]{0,1,2:T(8,128)} %constant.82) | copy-start | bytes 12292
  36.9 25.4 %copy-start.1 = (u32[32]{0:T(128)S(1)}, u32[32]{0:T(128)}, u32[]{:S(2)}) copy-start(u32[32]{0:T(128)} %constant.80) | copy-start | bytes 388
  50.4 1.4 collective-permute-start
  51.8 5.5 %collective-permute-start.1 = (bf16[32,1792]{1,0:T(8,128)(2,1)S(1)}, bf16[32,1792]{1,0:T(8,128)(2,1)S(1)}, u32[]{:S(2)}, u32[]{:S(2)}) collective-permute-start(bf16[32,1792]{1,0:T(8,128)(2,1)S(1)} %fusion.7), channel_id=1, source_target_pairs={{0,2},{1,3},{2,0},{3,1},{4,6},{5,7},{6,4},{7,5},{8,10},{9,11},{10,... | collective-permute-start | bytes 344072 | tf_op jit(solution)/shard_map/ppermute | solution.py:13
  57.4 4.9 %collective-permute-start.2 = (bf16[32,1792]{1,0:T(8,128)(2,1)S(1)}, bf16[32,1792]{1,0:T(8,128)(2,1)S(1)}, u32[]{:S(2)}, u32[]{:S(2)}) collective-permute-start(bf16[32,1792]{1,0:T(8,128)(2,1)S(1)} %get-tuple-element.5), channel_id=1, source_target_pairs={{0,4},{1,5},{2,6},{3,7},{4,0},{5,1},{6,2},{7,3},{8,12},{9,13},{10,... | collective-permute-start | bytes 344072 | tf_op jit(solution)/shard_map/ppermute | solution.py:13
  62.3 6.8 %collective-permute-start.3 = (bf16[32,1792]{1,0:T(8,128)(2,1)S(1)}, bf16[32,1792]{1,0:T(8,128)(2,1)S(1)}, u32[]{:S(2)}, u32[]{:S(2)}) collective-permute-start(bf16[32,1792]{1,0:T(8,128)(2,1)S(1)} %fusion.6), channel_id=1, source_target_pairs={{0,8},{1,9},{2,10},{3,11},{4,12},{5,13},{6,14},{7,15},{8,0},{9,1},... | collective-permute-start | bytes 344072 | tf_op jit(solution)/shard_map/ppermute | solution.py:13
where the time goes:
time: 151 us
  blocking collectives  94 us (62%)
  matrix products  36.7 us (24%)
  waiting for transfers between devices  16.5 us (11%)
  local copies, waits for them, and re-layouts  2 us (1%)
    unnamed x1, blocking collectives  69.2 us
    all_gather x1, blocking collectives, per_device(): piece = lax.all_gather(tokens, 'tensor', axis=0, tiled=True)  24.8 us
    ppermute x4, waiting for transfers between devices, swapped(): return lax.ppermute(value, axis, pairs)  16.5 us
    dot_general x1, matrix products, per_device(): up = jnp.dot(piece, up_weight, preferred_element_type=jnp.float32)  12 us
    dot_general x1, matrix products, per_device(): terms = jnp.dot(rotated, down_weight, preferred_element_type=jnp.float32)  11.9 us
    dot_general x1, matrix products, per_device(): gate = jnp.dot(piece, gate_weight, preferred_element_type=jnp.float32)  11.9 us
  transfers between devices with their start and end apart: 4, of which 4 were waited for; matrix products, arithmetic and copies ran while one was open for 0% of the time, Pallas kernels for 0%

commit v1 on v0

--- a/solution.py
+++ b/solution.py
@@ -1,10 +1,21 @@
+import functools
+
 import jax
 import jax.numpy as jnp
 import numpy as np
 from jax import lax
+from jax.experimental import pallas as pl
+from jax.experimental.pallas import tpu as pltpu
 from jax.sharding import PartitionSpec as P
 
 BLOCK = 32
+COLS = 256
+PAIRS = 4
+SPLIT = 4
+DOWNS = 6
+CHUNKS = 4
+LAG = 2
+MESH = pl.DeviceIdType.MESH
 
 
 def swapped(value, axis, stride):
@@ -22,7 +33,7 @@
     return (1 - 2 * parity).astype(np.float32)
 
 
-def per_device(tokens, gate_weight, up_weight, down_weight):
+def plain(tokens, gate_weight, up_weight, down_weight):
     devices = lax.axis_size("tensor")
     width = gate_weight.shape[1]
     scale = 1.0 / np.sqrt(devices * BLOCK)
@@ -49,6 +60,391 @@
     return mixed.astype(jnp.bfloat16)
 
 
+def parity(value, bits):
+    total = value & 1
+    for shift in range(1, bits):
+        total = total ^ ((value >> shift) & 1)
+    return total
+
+
+def kernel(
+    n,
+    tokens,
+    gate,
+    up,
+    down,
+    out,
+    gathered,
+    lhs,
+    acc,
+    weights,
+    downs,
+    signs,
+    rows,
+    first_out,
+    first_in,
+    second_out,
+    second_in,
+    half_out,
+    half_in,
+    quarter_out,
+    quarter_in,
+    piece_out,
+    piece_in,
+    weight_sem,
+    down_sem,
+    gather_send,
+    gather_recv,
+    turn_send,
+    turn_recv,
+    sum_send,
+    sum_recv,
+):
+    f32, bf16 = jnp.float32, jnp.bfloat16
+    me = lax.axis_index("tensor")
+    own, depth = tokens.shape
+    total = n * own
+    width = gate.shape[1]
+    blocks = width // COLS
+    outs = down.shape[1]
+    bits = n.bit_length() - 1
+    ring = n // 4
+    scale = float(1.0 / np.sqrt(n * BLOCK))
+    offset = [(i % ring) * 4 + (i // ring % 2) * 2 + i // (2 * ring) for i in range(n)]
+    part = depth // SPLIT
+
+    def weight_copy(which, b, piece):
+        slot = lax.rem(b, PAIRS)
+        source = (gate, up)[which]
+        return pltpu.make_async_copy(
+            source.at[pl.ds(piece * part, part), pl.ds(pl.multiple_of(b * COLS, COLS), COLS)],
+            weights.at[slot, which, pl.ds(piece * part, part)],
+            weight_sem.at[slot, which, piece],
+        )
+
+    def down_copy(b):
+        slot = lax.rem(b, DOWNS)
+        return pltpu.make_async_copy(
+            down.at[pl.ds(pl.multiple_of(b * COLS, COLS), COLS)], downs.at[slot], down_sem.at[slot]
+        )
+
+    def start_weights(b):
+        for piece in range(SPLIT):
+            for which in range(2):
+                weight_copy(which, b, piece).start()
+
+    for b in range(min(PAIRS, blocks)):
+        start_weights(jnp.int32(b))
+
+    barrier = pltpu.get_barrier_semaphore()
+    for i in range(1, n):
+        pl.semaphore_signal(barrier, inc=1, device_id={"tensor": me ^ offset[i]}, device_id_type=MESH)
+    pl.semaphore_wait(barrier, n - 1)
+
+    def pass_on(source, slot, mask):
+        return pltpu.make_async_remote_copy(
+            src_ref=source,
+            dst_ref=gathered.at[slot],
+            send_sem=gather_send.at[slot],
+            recv_sem=gather_recv.at[slot],
+            device_id={"tensor": me ^ mask},
+            device_id_type=MESH,
+        )
+
+    sends = []
+
+    def send(source, slot, mask):
+        copy = pass_on(source, slot, mask)
+        copy.start()
+        sends.append(copy)
+
+    for i in range(1, ring):
+        send(tokens, i, offset[i])
+    send(tokens, ring, 2)
+    send(tokens, 2 * ring, 1)
+
+    one = lax.broadcasted_iota(jnp.int32, (COLS, COLS), 0)
+    two = lax.broadcasted_iota(jnp.int32, (COLS, COLS), 1)
+    sign = (1 - 2 * parity(one & two & (BLOCK - 1), BLOCK.bit_length() - 1)).astype(f32)
+    signs[...] = jnp.where((one // BLOCK) == (two // BLOCK), sign, 0.0).astype(bf16)
+
+    order = [ring]
+    for i in range(1, ring):
+        order.append(i)
+        if i > 1:
+            order.append(ring + i - 1)
+    if ring > 1:
+        order.append(2 * ring - 1)
+    for i in order:
+        pass_on(gathered.at[i], i, 1).wait_recv()
+        if i < ring:
+            send(gathered.at[i], ring + i, 2)
+        send(gathered.at[i], 2 * ring + i, 1)
+    for i in range(2 * ring, n):
+        pass_on(gathered.at[i], i, 1).wait_recv()
+
+    @pl.loop(0, depth // 1024)
+    def _(c):
+        columns = pl.ds(pl.multiple_of(c * 1024, 1024), 1024)
+        for i in range(n):
+            value = tokens[:, columns] if i == 0 else gathered[i, :, columns]
+            acc[i * own : (i + 1) * own, columns] = value.astype(f32)
+        lhs[:, columns] = acc[:, columns].astype(bf16)
+
+    def exchange(source, target, which, b):
+        return [
+            pltpu.make_async_remote_copy(
+                src_ref=source.at[b, i],
+                dst_ref=target.at[b, i],
+                send_sem=turn_send.at[which, b],
+                recv_sem=turn_recv.at[which, b],
+                device_id={"tensor": me ^ offset[i]},
+                device_id_type=MESH,
+            )
+            for i in range(1, n)
+        ]
+
+    def all_of(source, target, which, b):
+        return pltpu.make_async_remote_copy(
+            src_ref=source.at[b, pl.ds(1, n - 1)],
+            dst_ref=target.at[b, pl.ds(1, n - 1)],
+            send_sem=turn_send.at[which, b],
+            recv_sem=turn_recv.at[which, b],
+            device_id={"tensor": me ^ 1},
+            device_id_type=MESH,
+        )
+
+    flips = [(1 - 2 * parity(me & offset[i], bits)).astype(f32) for i in range(n)]
+    whole = (1 - 2 * parity(me, bits)).astype(f32) * scale
+
+    def across(b):
+        all_of(first_out, first_in, 0, b).wait_recv()
+        values = [first_in[b, i].astype(f32) * flips[i] for i in range(n)]
+        step = 1
+        while step < n:
+            for i in range(n):
+                if not i & step:
+                    low, high = values[i], values[i + step]
+                    values[i], values[i + step] = low + high, low - high
+            step *= 2
+        for i in range(n):
+            target = second_in if i == 0 else second_out
+            target[b, i] = (values[i] * (flips[i] * whole)).astype(bf16)
+        for copy in exchange(second_out, second_in, 1, b):
+            copy.start()
+
+    @pl.loop(0, blocks)
+    def _(b):
+        slot = lax.rem(b, PAIRS)
+        sums = [jnp.zeros((total, COLS), f32) for _ in range(2)]
+        for piece in range(SPLIT):
+            rows_of = pl.ds(piece * part, part)
+            for which in range(2):
+                weight_copy(which, b, piece).wait()
+                sums[which] += jnp.dot(
+                    lhs[:, rows_of], weights[slot, which, rows_of], preferred_element_type=f32
+                )
+
+        @pl.when(b + PAIRS < blocks)
+        def _():
+            start_weights(b + PAIRS)
+
+        for e in range(pl.cdiv(DOWNS, PAIRS)):
+            index = (b - max(blocks - PAIRS, 0)) * pl.cdiv(DOWNS, PAIRS) + e
+
+            @pl.when((b + PAIRS >= blocks) & (index < min(DOWNS, blocks)))
+            def _():
+                down_copy(index).start()
+
+        hidden = sums[0] / (1.0 + jnp.exp(-sums[0])) * sums[1]
+        high = hidden.astype(bf16)
+        low = (hidden - high.astype(f32)).astype(bf16)
+        rows[...] = jnp.dot(high, signs[...], preferred_element_type=f32) + jnp.dot(
+            low, signs[...], preferred_element_type=f32
+        )
+        for i in range(n):
+            target = first_in if i == 0 else first_out
+            target[b, i] = rows[i * own : (i + 1) * own, :].astype(bf16)
+        for copy in exchange(first_out, first_in, 0, b):
+            copy.start()
+
+        @pl.when(b >= LAG)
+        def _():
+            across(b - LAG)
+
+    def rotated(b):
+        all_of(second_out, second_in, 1, b).wait_recv()
+        for i in range(n):
+            rows[i * own : (i + 1) * own, :] = second_in[b, i].astype(f32)
+        down_copy(jnp.int32(b)).wait()
+        return rows[...].astype(bf16)
+
+    pending = list(range(max(blocks - LAG, 0), blocks))
+    for b in range(blocks - 1):
+        if pending and (b >= 1 or blocks - 1 - b <= len(pending)):
+            if pending[0] != blocks - 1 or b >= 3 or b == blocks - 2:
+                across(pending.pop(0))
+        value = rotated(b)
+
+        @pl.loop(0, outs // 1024)
+        def _(c):
+            columns = pl.ds(pl.multiple_of(c * 1024, 1024), 1024)
+            term = jnp.dot(value, downs[b % DOWNS, :, columns], preferred_element_type=f32)
+            if b:
+                term = acc[:, columns] + term
+            acc[:, columns] = term
+
+        if b + DOWNS < blocks:
+            down_copy(jnp.int32(b + DOWNS)).start()
+    while pending:
+        across(pending.pop(0))
+
+    size = outs // CHUNKS
+    half, quarter = total // 2, total // 4
+
+    def sum_copy(level, c, source, target, mask, send_sem, recv_sem):
+        return pltpu.make_async_remote_copy(
+            src_ref=source,
+            dst_ref=target,
+            send_sem=send_sem,
+            recv_sem=recv_sem,
+            device_id={"tensor": me ^ mask},
+            device_id_type=MESH,
+        )
+
+    def half_copy(c):
+        return sum_copy(0, c, half_out.at[c], half_in.at[c], 1, sum_send.at[0, c], sum_recv.at[0, c])
+
+    def quarter_copy(c):
+        return sum_copy(
+            1, c, quarter_out.at[c], quarter_in.at[c], 2, sum_send.at[1, c], sum_recv.at[1, c]
+        )
+
+    def piece_copy(c, i):
+        return sum_copy(
+            2,
+            c,
+            piece_out.at[c, i - 1],
+            piece_in.at[c, i - 1],
+            offset[i],
+            sum_send.at[1 + i, c],
+            sum_recv.at[1 + i, c],
+        )
+
+    last = rotated(blocks - 1)
+    for c in range(CHUNKS):
+        columns = pl.ds(c * size, size)
+        term = jnp.dot(last, downs[(blocks - 1) % DOWNS, :, columns], preferred_element_type=f32)
+        if blocks > 1:
+            term = acc[:, columns] + term
+        half_out[c] = term[half:].astype(bf16)
+        acc[:half, columns] = term[:half]
+        half_copy(c).start()
+    for c in range(CHUNKS):
+        columns = pl.ds(c * size, size)
+        half_copy(c).wait_recv()
+        term = acc[:half, columns] + half_in[c].astype(f32)
+        quarter_out[c] = term[quarter:].astype(bf16)
+        acc[:quarter, columns] = term[:quarter]
+        quarter_copy(c).start()
+    for c in range(CHUNKS):
+        columns = pl.ds(c * size, size)
+        quarter_copy(c).wait_recv()
+        acc[:quarter, columns] = acc[:quarter, columns] + quarter_in[c].astype(f32)
+        for i in range(1, ring):
+            piece_out[c, i - 1] = acc[i * own : (i + 1) * own, columns].astype(bf16)
+            piece_copy(c, i).start()
+    for c in range(CHUNKS):
+        columns = pl.ds(c * size, size)
+        term = acc[:own, columns]
+        for i in range(1, ring):
+            piece_copy(c, i).wait_recv()
+            term = term + piece_in[c, i - 1].astype(f32)
+        out[:, columns] = term.astype(bf16)
+
+    for copy in sends:
+        copy.wait_send()
+    for b in range(blocks):
+        all_of(first_out, first_in, 0, b).wait_send()
+        all_of(second_out, second_in, 1, b).wait_send()
+    for c in range(CHUNKS):
+        half_copy(c).wait_send()
+        quarter_copy(c).wait_send()
+        for i in range(1, ring):
+            piece_copy(c, i).wait_send()
+
+
+def fused(n, tokens, gate_weight, up_weight, down_weight):
+    own, depth = tokens.shape
+    total = n * own
+    width = gate_weight.shape[1]
+    blocks = width // COLS
+    outs = down_weight.shape[1]
+    ring = n // 4
+    size = outs // CHUNKS
+    bf16, f32 = jnp.bfloat16, jnp.float32
+    turn = pltpu.VMEM((blocks, n, own, COLS), bf16)
+    vmem = pl.BlockSpec(memory_space=pltpu.VMEM)
+    anywhere = pl.BlockSpec(memory_space=pl.ANY)
+    return pl.pallas_call(
+        functools.partial(kernel, n),
+        out_shape=jax.ShapeDtypeStruct((own, outs), bf16),
+        in_specs=[vmem, anywhere, anywhere, anywhere],
+        out_specs=vmem,
+        scratch_shapes=[
+            pltpu.VMEM((n, own, depth), bf16),
+            pltpu.VMEM((total, depth), bf16),
+            pltpu.VMEM((total, max(outs, depth)), f32),
+            pltpu.VMEM((PAIRS, 2, depth, COLS), bf16),
+            pltpu.VMEM((DOWNS, COLS, outs), bf16),
+            pltpu.VMEM((COLS, COLS), bf16),
+            pltpu.VMEM((total, COLS), f32),
+            turn,
+            turn,
+            turn,
+            turn,
+            pltpu.VMEM((CHUNKS, total // 2, size), bf16),
+            pltpu.VMEM((CHUNKS, total // 2, size), bf16),
+            pltpu.VMEM((CHUNKS, total // 4, size), bf16),
+            pltpu.VMEM((CHUNKS, total // 4, size), bf16),
+            pltpu.VMEM((CHUNKS, ring - 1, own, size), bf16),
+            pltpu.VMEM((CHUNKS, ring - 1, own, size), bf16),
+            pltpu.SemaphoreType.DMA((PAIRS, 2, SPLIT)),
+            pltpu.SemaphoreType.DMA((DOWNS,)),
+            pltpu.SemaphoreType.DMA((n,)),
+            pltpu.SemaphoreType.DMA((n,)),
+            pltpu.SemaphoreType.DMA((2, blocks)),
+            pltpu.SemaphoreType.DMA((2, blocks)),
+            pltpu.SemaphoreType.DMA((1 + ring, CHUNKS)),
+            pltpu.SemaphoreType.DMA((1 + ring, CHUNKS)),
+        ],
+        compiler_params=pltpu.CompilerParams(
+            collective_id=0, has_side_effects=True, vmem_limit_bytes=67_000_000
+        ),
+    )(tokens, gate_weight, up_weight, down_weight)
+
+
+def per_device(tokens, gate_weight, up_weight, down_weight):
+    n = lax.axis_size("tensor")
+    own, depth = tokens.shape
+    width, outs = gate_weight.shape[1], down_weight.shape[1]
+    held = 2 * COLS * (2 * PAIRS * depth + DOWNS * outs)
+    fits = (
+        8 <= n
+        and n & (n - 1) == 0
+        and width % COLS == 0
+        and width // COLS > max(PAIRS, LAG)
+        and n * own % 32 == 0
+        and n * own <= 64
+        and depth % (1024 * SPLIT) == 0
+        and outs % (1024 * CHUNKS) == 0
+        and held <= 60 << 20
+    )
+    if fits:
+        return fused(n, tokens, gate_weight, up_weight, down_weight)
+    return plain(tokens, gate_weight, up_weight, down_weight)
+
+
 def solution(mesh):
     return jax.shard_map(
         per_device,

time: 151 us -> 60.1 us (0.40)
  blocking collectives: 94 us -> 0 us
  Pallas kernels: 0 us -> 58.4 us
  matrix products: 36.7 us -> 0 us
  waiting for transfers between devices: 16.5 us -> 0 us
    unnamed x1 -> x0, blocking collectives: 69.2 us -> none
    pallas_call x0 -> x1, Pallas kernels: none -> 58.4 us  [fused(): pl.pallas_call(functools.partial(kernel, n), out_shape=jax.ShapeDtypeStru...]
    dot_general x4 -> x0, matrix products: 36.7 us -> none  [the longest x1 12 us: per_device(): up = jnp.dot(piece, up_weight, preferred_element_type=jnp.float32)]
    all_gather x1 -> x0, blocking collectives: 24.8 us -> none  [per_device(): piece = lax.all_gather(tokens, 'tensor', axis=0, tiled=True)]
    ppermute x4 -> x0, waiting for transfers between devices: 16.5 us -> none  [swapped(): return lax.ppermute(value, axis, pairs)]
  transfers between devices with their start and end apart: 4 -> 0, of which waited for: 4 -> 0; matrix products, arithmetic and copies ran while one was open for 0% -> 0% of each run, Pallas kernels for 0% -> 0%
where the time goes in v1:
time: 60.1 us; the launch traced here: 59.8 us
  Pallas kernels  58.4 us (97%)
  local copies, waits for them, and re-layouts  1.4 us (2%)
    pallas_call x1, Pallas kernels, fused(): pl.pallas_call(functools.partial(kernel, n), out_shape=jax.ShapeDtypeStru...  58.4 us
    unnamed x1, local copies, waits for them, and re-layouts  1.4 us

profile of v1, /device:TPU:0, one launch (start us, length us, event | category | flops | bytes accessed | tf_op | source)
XLA Modules:
  0.0 59.8 jit_solution(18303208846073067578)
XLA Ops:
  0.0 58.4 %shard_map.46 = bf16[2,8192]{1,0:T(2,128)(2,1)} custom-call(bf16[2,8192]{1,0:T(2,128)(2,1)} %tokens.1, bf16[8192,1792]{1,0:T(8,128)(2,1)} %gate.1, bf16[8192,1792]{1,0:T(8,128)(2,1)} %up.1, bf16[1792,8192]{1,0:T(8,128)(2,1)} %down.1), custom_call_target="tpu_custom_call" | custom-call | tf_op jit(solution)/shard_map/pallas_call | solution.py:389
  58.4 1.4 %copy.6 = bf16[2,8192]{1,0:T(2,128)(2,1)} copy(bf16[2,8192]{1,0:T(2,128)(2,1)} %shard_map.46) | data formatting | bytes 65536

commit v2 on v1

--- a/solution.py
+++ b/solution.py
@@ -14,6 +14,7 @@
 SPLIT = 4
 DOWNS = 6
 CHUNKS = 4
+GROUP = 3
 LAG = 2
 MESH = pl.DeviceIdType.MESH
 
@@ -135,6 +136,8 @@
 
     for b in range(min(PAIRS, blocks)):
         start_weights(jnp.int32(b))
+    for b in range(min(DOWNS, blocks)):
+        down_copy(jnp.int32(b)).start()
 
     barrier = pltpu.get_barrier_semaphore()
     for i in range(1, n):
@@ -191,25 +194,31 @@
             acc[i * own : (i + 1) * own, columns] = value.astype(f32)
         lhs[:, columns] = acc[:, columns].astype(bf16)
 
-    def exchange(source, target, which, b):
+    groups = [(lo, min(lo + GROUP, blocks)) for lo in range(0, blocks, GROUP)]
+
+    def exchange(source, target, which, g):
+        lo, hi = groups[g]
+        columns = pl.ds(lo * COLS, (hi - lo) * COLS)
         return [
             pltpu.make_async_remote_copy(
-                src_ref=source.at[b, i],
-                dst_ref=target.at[b, i],
-                send_sem=turn_send.at[which, b],
-                recv_sem=turn_recv.at[which, b],
+                src_ref=source.at[i, :, columns],
+                dst_ref=target.at[i, :, columns],
+                send_sem=turn_send.at[which, g],
+                recv_sem=turn_recv.at[which, g],
                 device_id={"tensor": me ^ offset[i]},
                 device_id_type=MESH,
             )
             for i in range(1, n)
         ]
 
-    def all_of(source, target, which, b):
+    def all_of(source, target, which, g):
+        lo, hi = groups[g]
+        part_of = (pl.ds(1, n - 1), slice(None), pl.ds(lo * COLS, (hi - lo) * COLS))
         return pltpu.make_async_remote_copy(
-            src_ref=source.at[b, pl.ds(1, n - 1)],
-            dst_ref=target.at[b, pl.ds(1, n - 1)],
-            send_sem=turn_send.at[which, b],
-            recv_sem=turn_recv.at[which, b],
+            src_ref=source.at[part_of],
+            dst_ref=target.at[part_of],
+            send_sem=turn_send.at[which, g],
+            recv_sem=turn_recv.at[which, g],
             device_id={"tensor": me ^ 1},
             device_id_type=MESH,
         )
@@ -217,24 +226,25 @@
     flips = [(1 - 2 * parity(me & offset[i], bits)).astype(f32) for i in range(n)]
     whole = (1 - 2 * parity(me, bits)).astype(f32) * scale
 
-    def across(b):
-        all_of(first_out, first_in, 0, b).wait_recv()
-        values = [first_in[b, i].astype(f32) * flips[i] for i in range(n)]
-        step = 1
-        while step < n:
+    def across(g):
+        all_of(first_out, first_in, 0, g).wait_recv()
+        for b in range(*groups[g]):
+            columns = pl.ds(b * COLS, COLS)
+            values = [first_in[i, :, columns].astype(f32) * flips[i] for i in range(n)]
+            step = 1
+            while step < n:
+                for i in range(n):
+                    if not i & step:
+                        low, high = values[i], values[i + step]
+                        values[i], values[i + step] = low + high, low - high
+                step *= 2
             for i in range(n):
-                if not i & step:
-                    low, high = values[i], values[i + step]
-                    values[i], values[i + step] = low + high, low - high
-            step *= 2
-        for i in range(n):
-            target = second_in if i == 0 else second_out
-            target[b, i] = (values[i] * (flips[i] * whole)).astype(bf16)
-        for copy in exchange(second_out, second_in, 1, b):
+                target = second_in if i == 0 else second_out
+                target[i, :, columns] = (values[i] * (flips[i] * whole)).astype(bf16)
+        for copy in exchange(second_out, second_in, 1, g):
             copy.start()
 
-    @pl.loop(0, blocks)
-    def _(b):
+    def block(b):
         slot = lax.rem(b, PAIRS)
         sums = [jnp.zeros((total, COLS), f32) for _ in range(2)]
         for piece in range(SPLIT):
@@ -249,13 +259,6 @@
         def _():
             start_weights(b + PAIRS)
 
-        for e in range(pl.cdiv(DOWNS, PAIRS)):
-            index = (b - max(blocks - PAIRS, 0)) * pl.cdiv(DOWNS, PAIRS) + e
-
-            @pl.when((b + PAIRS >= blocks) & (index < min(DOWNS, blocks)))
-            def _():
-                down_copy(index).start()
-
         hidden = sums[0] / (1.0 + jnp.exp(-sums[0])) * sums[1]
         high = hidden.astype(bf16)
         low = (hidden - high.astype(f32)).astype(bf16)
@@ -264,26 +267,43 @@
         )
         for i in range(n):
             target = first_in if i == 0 else first_out
-            target[b, i] = rows[i * own : (i + 1) * own, :].astype(bf16)
-        for copy in exchange(first_out, first_in, 0, b):
-            copy.start()
-
-        @pl.when(b >= LAG)
-        def _():
-            across(b - LAG)
+            target[i, :, pl.ds(pl.multiple_of(b * COLS, COLS), COLS)] = rows[
+                i * own : (i + 1) * own, :
+            ].astype(bf16)
+
+    begun = 0
+    waiting = []
+    for b in range(blocks):
+        ends = [g for g, (_, hi) in enumerate(groups) if hi == b + 1]
+        due = [g for g in waiting if groups[g][1] + LAG <= b + 1]
+        if ends or due or b == blocks - 1:
+            pl.loop(begun, b + 1)(block)
+            begun = b + 1
+        for g in ends:
+            for copy in exchange(first_out, first_in, 0, g):
+                copy.start()
+            waiting.append(g)
+        for g in due:
+            across(g)
+            waiting.remove(g)
 
     def rotated(b):
-        all_of(second_out, second_in, 1, b).wait_recv()
+        g = b // GROUP
+        if b == groups[g][0]:
+            all_of(second_out, second_in, 1, g).wait_recv()
+        columns = pl.ds(b * COLS, COLS)
         for i in range(n):
-            rows[i * own : (i + 1) * own, :] = second_in[b, i].astype(f32)
+            rows[i * own : (i + 1) * own, :] = second_in[i, :, columns].astype(f32)
         down_copy(jnp.int32(b)).wait()
         return rows[...].astype(bf16)
 
-    pending = list(range(max(blocks - LAG, 0), blocks))
-    for b in range(blocks - 1):
-        if pending and (b >= 1 or blocks - 1 - b <= len(pending)):
-            if pending[0] != blocks - 1 or b >= 3 or b == blocks - 2:
-                across(pending.pop(0))
+    last_group = groups[-1][0]
+    while len(waiting) > 1:
+        across(waiting.pop(0))
+    early = max(last_group - 1, blocks - DOWNS)
+    for b in range(early):
+        if waiting and b == min(2, early - 1):
+            across(waiting.pop(0))
         value = rotated(b)
 
         @pl.loop(0, outs // 1024)
@@ -296,8 +316,8 @@
 
         if b + DOWNS < blocks:
             down_copy(jnp.int32(b + DOWNS)).start()
-    while pending:
-        across(pending.pop(0))
+    while waiting:
+        across(waiting.pop(0))
 
     size = outs // CHUNKS
     half, quarter = total // 2, total // 4
@@ -331,12 +351,12 @@
             sum_recv.at[1 + i, c],
         )
 
-    last = rotated(blocks - 1)
+    last = [(b, rotated(b)) for b in range(early, blocks)]
     for c in range(CHUNKS):
         columns = pl.ds(c * size, size)
-        term = jnp.dot(last, downs[(blocks - 1) % DOWNS, :, columns], preferred_element_type=f32)
-        if blocks > 1:
-            term = acc[:, columns] + term
+        term = acc[:, columns]
+        for b, value in last:
+            term = term + jnp.dot(value, downs[b % DOWNS, :, columns], preferred_element_type=f32)
         half_out[c] = term[half:].astype(bf16)
         acc[:half, columns] = term[:half]
         half_copy(c).start()
@@ -364,9 +384,9 @@
 
     for copy in sends:
         copy.wait_send()
-    for b in range(blocks):
-        all_of(first_out, first_in, 0, b).wait_send()
-        all_of(second_out, second_in, 1, b).wait_send()
+    for g in range(len(groups)):
+        all_of(first_out, first_in, 0, g).wait_send()
+        all_of(second_out, second_in, 1, g).wait_send()
     for c in range(CHUNKS):
         half_copy(c).wait_send()
         quarter_copy(c).wait_send()
@@ -383,7 +403,7 @@
     ring = n // 4
     size = outs // CHUNKS
     bf16, f32 = jnp.bfloat16, jnp.float32
-    turn = pltpu.VMEM((blocks, n, own, COLS), bf16)
+    turn = pltpu.VMEM((n, own, width), bf16)
     vmem = pl.BlockSpec(memory_space=pltpu.VMEM)
     anywhere = pl.BlockSpec(memory_space=pl.ANY)
     return pl.pallas_call(
@@ -413,8 +433,8 @@
             pltpu.SemaphoreType.DMA((DOWNS,)),
             pltpu.SemaphoreType.DMA((n,)),
             pltpu.SemaphoreType.DMA((n,)),
-            pltpu.SemaphoreType.DMA((2, blocks)),
-            pltpu.SemaphoreType.DMA((2, blocks)),
+            pltpu.SemaphoreType.DMA((2, pl.cdiv(blocks, GROUP))),
+            pltpu.SemaphoreType.DMA((2, pl.cdiv(blocks, GROUP))),
             pltpu.SemaphoreType.DMA((1 + ring, CHUNKS)),
             pltpu.SemaphoreType.DMA((1 + ring, CHUNKS)),
         ],
@@ -433,7 +453,7 @@
         8 <= n
         and n & (n - 1) == 0
         and width % COLS == 0
-        and width // COLS > max(PAIRS, LAG)
+        and width // COLS > max(PAIRS, LAG, GROUP, DOWNS)
         and n * own % 32 == 0
         and n * own <= 64
         and depth % (1024 * SPLIT) == 0

time: 60.1 us -> 59.8 us (level)
  no operation moved by 1% of the time
where the time goes in v2:
time: 59.8 us; the launch traced here: 59.6 us
  Pallas kernels  58.2 us (97%)
  local copies, waits for them, and re-layouts  1.4 us (2%)
    pallas_call x1, Pallas kernels, fused(): pl.pallas_call(functools.partial(kernel, n), out_shape=jax.ShapeDtypeStru...  58.2 us
    unnamed x1, local copies, waits for them, and re-layouts  1.4 us

profile of v2, /device:TPU:0, one launch (start us, length us, event | category | flops | bytes accessed | tf_op | source)
XLA Modules:
  0.0 59.6 jit_solution(4972554568301487883)
XLA Ops:
  0.0 58.2 %shard_map.46 = bf16[2,8192]{1,0:T(2,128)(2,1)} custom-call(bf16[2,8192]{1,0:T(2,128)(2,1)} %tokens.1, bf16[8192,1792]{1,0:T(8,128)(2,1)} %gate.1, bf16[8192,1792]{1,0:T(8,128)(2,1)} %up.1, bf16[1792,8192]{1,0:T(8,128)(2,1)} %down.1), custom_call_target="tpu_custom_call" | custom-call | tf_op jit(solution)/shard_map/pallas_call | solution.py:409
  58.2 1.4 %copy.6 = bf16[2,8192]{1,0:T(2,128)(2,1)} copy(bf16[2,8192]{1,0:T(2,128)(2,1)} %shard_map.46) | data formatting | bytes 65536

commit v3 on v2

--- a/solution.py
+++ b/solution.py
@@ -119,7 +119,7 @@
         source = (gate, up)[which]
         return pltpu.make_async_copy(
             source.at[pl.ds(piece * part, part), pl.ds(pl.multiple_of(b * COLS, COLS), COLS)],
-            weights.at[slot, which, pl.ds(piece * part, part)],
+            weights.at[slot, pl.ds(piece * part, part), pl.ds(which * COLS, COLS)],
             weight_sem.at[slot, which, piece],
         )
 
@@ -246,20 +246,19 @@
 
     def block(b):
         slot = lax.rem(b, PAIRS)
-        sums = [jnp.zeros((total, COLS), f32) for _ in range(2)]
+        sums = jnp.zeros((total, 2 * COLS), f32)
         for piece in range(SPLIT):
             rows_of = pl.ds(piece * part, part)
             for which in range(2):
                 weight_copy(which, b, piece).wait()
-                sums[which] += jnp.dot(
-                    lhs[:, rows_of], weights[slot, which, rows_of], preferred_element_type=f32
-                )
+            sums += jnp.dot(lhs[:, rows_of], weights[slot, rows_of, :], preferred_element_type=f32)
 
         @pl.when(b + PAIRS < blocks)
         def _():
             start_weights(b + PAIRS)
 
-        hidden = sums[0] / (1.0 + jnp.exp(-sums[0])) * sums[1]
+        left, right = sums[:, :COLS], sums[:, COLS:]
+        hidden = left / (1.0 + jnp.exp(-left)) * right
         high = hidden.astype(bf16)
         low = (hidden - high.astype(f32)).astype(bf16)
         rows[...] = jnp.dot(high, signs[...], preferred_element_type=f32) + jnp.dot(
@@ -415,7 +414,7 @@
             pltpu.VMEM((n, own, depth), bf16),
             pltpu.VMEM((total, depth), bf16),
             pltpu.VMEM((total, max(outs, depth)), f32),
-            pltpu.VMEM((PAIRS, 2, depth, COLS), bf16),
+            pltpu.VMEM((PAIRS, depth, 2 * COLS), bf16),
             pltpu.VMEM((DOWNS, COLS, outs), bf16),
             pltpu.VMEM((COLS, COLS), bf16),
             pltpu.VMEM((total, COLS), f32),

time: 59.8 us -> 54.3 us (0.908)
  Pallas kernels: 58.2 us -> 52.6 us
    pallas_call x1, Pallas kernels: 58.2 us -> 52.6 us  [fused(): pl.pallas_call(functools.partial(kernel, n), out_shape=jax.ShapeDtypeStru...]
where the time goes in v3:
time: 54.3 us; the launch traced here: 54 us
  Pallas kernels  52.6 us (97%)
  local copies, waits for them, and re-layouts  1.4 us (3%)
    pallas_call x1, Pallas kernels, fused(): pl.pallas_call(functools.partial(kernel, n), out_shape=jax.ShapeDtypeStru...  52.6 us
    unnamed x1, local copies, waits for them, and re-layouts  1.4 us

profile of v3, /device:TPU:0, one launch (start us, length us, event | category | flops | bytes accessed | tf_op | source)
XLA Modules:
  0.0 54.0 jit_solution(8072982389890287334)
XLA Ops:
  0.0 52.6 %shard_map.46 = bf16[2,8192]{1,0:T(2,128)(2,1)} custom-call(bf16[2,8192]{1,0:T(2,128)(2,1)} %tokens.1, bf16[8192,1792]{1,0:T(8,128)(2,1)} %gate.1, bf16[8192,1792]{1,0:T(8,128)(2,1)} %up.1, bf16[1792,8192]{1,0:T(8,128)(2,1)} %down.1), custom_call_target="tpu_custom_call" | custom-call | tf_op jit(solution)/shard_map/pallas_call | solution.py:408
  52.6 1.4 %copy.6 = bf16[2,8192]{1,0:T(2,128)(2,1)} copy(bf16[2,8192]{1,0:T(2,128)(2,1)} %shard_map.46) | data formatting | bytes 65536
